TPU v7x, 128 devices: a whole 4x4x4 slice. The times are simulated.
128 devices in a mesh: op: 16 (over z_lo, y, core), sec: 8 (over z_hi, x).
Axes of the slice: x: 4, y: 4, z: 4 (z_hi: 2, z_lo: 2; z = z_hi * 2 + z_lo), core: 2. Of those that a mesh axis runs over, the one named last changes fastest.
Arguments:
- wavefunction: bfloat16 [3, 8, 512, 512], P(None, 'sec'), may hold values from -6 to 6
- left_ops: bfloat16 [256, 512, 512], P('op'), may hold values from -0.015625 to 0.015625
- right_ops: bfloat16 [256, 512, 512], P('op'), may hold values from -0.25 to 0.25
- targets: int32 [256, 8], P('op'), may hold values from 0 to 7, each once within a row
Outputs:
- sigma: bfloat16 [3, 8, 512, 512], P(None, 'sec', 'op')
Inputs may be any that keep to these rules, and one draw needn't show every extreme that they name: Each row of targets names every sector exactly once.
All inputs are finite; a program needn't handle non-finite values.
Results may differ from a plain program's by a relative error of at most 0.005.
Values may be sent and summed in bfloat16 or wider, within the bound.
A program may use at most 192 MiB of HBM per device.

v0:
```python
import jax
import jax.numpy as jnp
from jax import lax
from jax.sharding import PartitionSpec as P


def per_device(wavefunction, left_ops, right_ops, targets):
    vectors, sec_local, block_size, _ = wavefunction.shape
    sec_total = targets.shape[1]
    first_sector = lax.axis_index("sec") * sec_local
    owned_ids = lax.dynamic_slice_in_dim(targets, first_sector, sec_local, 1)

    def source_operator(accumulated, op_item):
        left_block, right_block, target_ids = op_item
        middle = jnp.einsum(
            "ab,vsbc->vsac", left_block, wavefunction, preferred_element_type=jnp.float32
        ).astype(jnp.bfloat16)
        contribution = jnp.einsum(
            "vsac,dc->vsad", middle, right_block, preferred_element_type=jnp.float32
        )
        return (accumulated.at[:, target_ids].add(contribution), None)

    start_value = jnp.zeros((vectors, sec_total, block_size, block_size), jnp.float32)
    partial_sums, _ = lax.scan(source_operator, start_value, (left_ops, right_ops, owned_ids))
    reduced = lax.psum_scatter(partial_sums, "op", scatter_dimension=2, tiled=True)
    summed = lax.psum_scatter(reduced, "sec", scatter_dimension=1, tiled=True)
    return summed.astype(jnp.bfloat16)


def solution(mesh):
    return jax.shard_map(
        per_device,
        mesh=mesh,
        in_specs=(
            P(None, "sec", None, None),
            P("op", None, None),
            P("op", None, None),
            P("op", None),
        ),
        out_specs=P(None, "sec", "op", None),
        check_vma=False,
    )
```

profile of v0, /device:TPU:0, one launch (start us, length us, event | category | flops | bytes accessed | tf_op | source)
XLA Modules:
  0.0 426.9 jit_solution(18314054211415966248)
XLA Ops:
  7.2 11.5 %broadcast_in_dim.4.clone = f32[3,8,512,512]{3,2,1,0:T(8,128)} broadcast(f32[]{:T(128)} %constant.43.clone.1), dimensions={} | broadcast | bytes 25165828 | tf_op jit(solution)/shard_map/broadcast_in_dim | solution.py:23
  18.8 174.1 %while.11 = (s32[]{:T(128)}, f32[3,8,512,512]{3,2,1,0:T(8,128)}, s32[16,1]{0,1:T(1,128)S(1)}, bf16[16,512,512]{2,1,0:T(8,128)(2,1)}, bf16[3,1,512,512]{3,2,0,1:T...) while((s32[]{:T(128)}, f32[3,8,512,512]{3,2,1,0:T(8,128)}, ...), condition=%wide.region_2.3_spmd, body=%wide.region_0.2_spmd.sunk | while | flops 1612972032 | bytes 15206576 | solution.py:24
  21.7 2.2 constant_dynamic-slice_fusion.6
  23.9 5.8 %fusion.25 = f32[3,8,512,512]{3,2,1,0:T(8,128)} fusion(f32[3,8,512,512]{3,2,1,0:T(8,128)} %get-tuple-element.122, s32[]{:T(128)} %bitcast.60, f32[3,1,512,512]{3,2,1,0:T(8,128)S(1)} %constant_dynamic-slice_fusion.6, pred[]{:T(512)} %and_reduce_fusion.2, bf16[3,1,512,512]{3,2,0,1:T(8,128)(2,1)} %get-tuple-element.135, ...), kind=kOutput, calls=%fused_computation.2.clone.1 | convolution fusion | flops 1612972032 | bytes 8914944 | tf_op jit(solution)/shard_map/while/body/eval_jaxpr/vsac,dc->vsad/dot_general | solution.py:18
  32.7 2.2 constant_dynamic-slice_fusion.6
  34.9 5.7 %fusion.25 = f32[3,8,512,512]{3,2,1,0:T(8,128)} fusion(f32[3,8,512,512]{3,2,1,0:T(8,128)} %get-tuple-element.122, s32[]{:T(128)} %bitcast.60, f32[3,1,512,512]{3,2,1,0:T(8,128)S(1)} %constant_dynamic-slice_fusion.6, pred[]{:T(512)} %and_reduce_fusion.2, bf16[3,1,512,512]{3,2,0,1:T(8,128)(2,1)} %get-tuple-element.135, ...), kind=kOutput, calls=%fused_computation.2.clone.1 | convolution fusion | flops 1612972032 | bytes 8914944 | tf_op jit(solution)/shard_map/while/body/eval_jaxpr/vsac,dc->vsad/dot_general | solution.py:18
  45.7 5.7 %fusion.25 = f32[3,8,512,512]{3,2,1,0:T(8,128)} fusion(f32[3,8,512,512]{3,2,1,0:T(8,128)} %get-tuple-element.122, s32[]{:T(128)} %bitcast.60, f32[3,1,512,512]{3,2,1,0:T(8,128)S(1)} %constant_dynamic-slice_fusion.6, pred[]{:T(512)} %and_reduce_fusion.2, bf16[3,1,512,512]{3,2,0,1:T(8,128)(2,1)} %get-tuple-element.135, ...), kind=kOutput, calls=%fused_computation.2.clone.1 | convolution fusion | flops 1612972032 | bytes 8914944 | tf_op jit(solution)/shard_map/while/body/eval_jaxpr/vsac,dc->vsad/dot_general | solution.py:18
  54.4 2.2 constant_dynamic-slice_fusion.6
  56.6 5.7 %fusion.25 = f32[3,8,512,512]{3,2,1,0:T(8,128)} fusion(f32[3,8,512,512]{3,2,1,0:T(8,128)} %get-tuple-element.122, s32[]{:T(128)} %bitcast.60, f32[3,1,512,512]{3,2,1,0:T(8,128)S(1)} %constant_dynamic-slice_fusion.6, pred[]{:T(512)} %and_reduce_fusion.2, bf16[3,1,512,512]{3,2,0,1:T(8,128)(2,1)} %get-tuple-element.135, ...), kind=kOutput, calls=%fused_computation.2.clone.1 | convolution fusion | flops 1612972032 | bytes 8914944 | tf_op jit(solution)/shard_map/while/body/eval_jaxpr/vsac,dc->vsad/dot_general | solution.py:18
  65.3 2.2 constant_dynamic-slice_fusion.6
  67.5 5.8 %fusion.25 = f32[3,8,512,512]{3,2,1,0:T(8,128)} fusion(f32[3,8,512,512]{3,2,1,0:T(8,128)} %get-tuple-element.122, s32[]{:T(128)} %bitcast.60, f32[3,1,512,512]{3,2,1,0:T(8,128)S(1)} %constant_dynamic-slice_fusion.6, pred[]{:T(512)} %and_reduce_fusion.2, bf16[3,1,512,512]{3,2,0,1:T(8,128)(2,1)} %get-tuple-element.135, ...), kind=kOutput, calls=%fused_computation.2.clone.1 | convolution fusion | flops 1612972032 | bytes 8914944 | tf_op jit(solution)/shard_map/while/body/eval_jaxpr/vsac,dc->vsad/dot_general | solution.py:18
  78.4 5.7 %fusion.25 = f32[3,8,512,512]{3,2,1,0:T(8,128)} fusion(f32[3,8,512,512]{3,2,1,0:T(8,128)} %get-tuple-element.122, s32[]{:T(128)} %bitcast.60, f32[3,1,512,512]{3,2,1,0:T(8,128)S(1)} %constant_dynamic-slice_fusion.6, pred[]{:T(512)} %and_reduce_fusion.2, bf16[3,1,512,512]{3,2,0,1:T(8,128)(2,1)} %get-tuple-element.135, ...), kind=kOutput, calls=%fused_computation.2.clone.1 | convolution fusion | flops 1612972032 | bytes 8914944 | tf_op jit(solution)/shard_map/while/body/eval_jaxpr/vsac,dc->vsad/dot_general | solution.py:18
  89.3 5.7 %fusion.25 = f32[3,8,512,512]{3,2,1,0:T(8,128)} fusion(f32[3,8,512,512]{3,2,1,0:T(8,128)} %get-tuple-element.122, s32[]{:T(128)} %bitcast.60, f32[3,1,512,512]{3,2,1,0:T(8,128)S(1)} %constant_dynamic-slice_fusion.6, pred[]{:T(512)} %and_reduce_fusion.2, bf16[3,1,512,512]{3,2,0,1:T(8,128)(2,1)} %get-tuple-element.135, ...), kind=kOutput, calls=%fused_computation.2.clone.1 | convolution fusion | flops 1612972032 | bytes 8914944 | tf_op jit(solution)/shard_map/while/body/eval_jaxpr/vsac,dc->vsad/dot_general | solution.py:18
  100.1 5.7 %fusion.25 = f32[3,8,512,512]{3,2,1,0:T(8,128)} fusion(f32[3,8,512,512]{3,2,1,0:T(8,128)} %get-tuple-element.122, s32[]{:T(128)} %bitcast.60, f32[3,1,512,512]{3,2,1,0:T(8,128)S(1)} %constant_dynamic-slice_fusion.6, pred[]{:T(512)} %and_reduce_fusion.2, bf16[3,1,512,512]{3,2,0,1:T(8,128)(2,1)} %get-tuple-element.135, ...), kind=kOutput, calls=%fused_computation.2.clone.1 | convolution fusion | flops 1612972032 | bytes 8914944 | tf_op jit(solution)/shard_map/while/body/eval_jaxpr/vsac,dc->vsad/dot_general | solution.py:18
  111.0 5.7 %fusion.25 = f32[3,8,512,512]{3,2,1,0:T(8,128)} fusion(f32[3,8,512,512]{3,2,1,0:T(8,128)} %get-tuple-element.122, s32[]{:T(128)} %bitcast.60, f32[3,1,512,512]{3,2,1,0:T(8,128)S(1)} %constant_dynamic-slice_fusion.6, pred[]{:T(512)} %and_reduce_fusion.2, bf16[3,1,512,512]{3,2,0,1:T(8,128)(2,1)} %get-tuple-element.135, ...), kind=kOutput, calls=%fused_computation.2.clone.1 | convolution fusion | flops 1612972032 | bytes 8914944 | tf_op jit(solution)/shard_map/while/body/eval_jaxpr/vsac,dc->vsad/dot_general | solution.py:18
  121.8 5.7 %fusion.25 = f32[3,8,512,512]{3,2,1,0:T(8,128)} fusion(f32[3,8,512,512]{3,2,1,0:T(8,128)} %get-tuple-element.122, s32[]{:T(128)} %bitcast.60, f32[3,1,512,512]{3,2,1,0:T(8,128)S(1)} %constant_dynamic-slice_fusion.6, pred[]{:T(512)} %and_reduce_fusion.2, bf16[3,1,512,512]{3,2,0,1:T(8,128)(2,1)} %get-tuple-element.135, ...), kind=kOutput, calls=%fused_computation.2.clone.1 | convolution fusion | flops 1612972032 | bytes 8914944 | tf_op jit(solution)/shard_map/while/body/eval_jaxpr/vsac,dc->vsad/dot_general | solution.py:18
  132.7 5.7 %fusion.25 = f32[3,8,512,512]{3,2,1,0:T(8,128)} fusion(f32[3,8,512,512]{3,2,1,0:T(8,128)} %get-tuple-element.122, s32[]{:T(128)} %bitcast.60, f32[3,1,512,512]{3,2,1,0:T(8,128)S(1)} %constant_dynamic-slice_fusion.6, pred[]{:T(512)} %and_reduce_fusion.2, bf16[3,1,512,512]{3,2,0,1:T(8,128)(2,1)} %get-tuple-element.135, ...), kind=kOutput, calls=%fused_computation.2.clone.1 | convolution fusion | flops 1612972032 | bytes 8914944 | tf_op jit(solution)/shard_map/while/body/eval_jaxpr/vsac,dc->vsad/dot_general | solution.py:18
  143.6 5.7 %fusion.25 = f32[3,8,512,512]{3,2,1,0:T(8,128)} fusion(f32[3,8,512,512]{3,2,1,0:T(8,128)} %get-tuple-element.122, s32[]{:T(128)} %bitcast.60, f32[3,1,512,512]{3,2,1,0:T(8,128)S(1)} %constant_dynamic-slice_fusion.6, pred[]{:T(512)} %and_reduce_fusion.2, bf16[3,1,512,512]{3,2,0,1:T(8,128)(2,1)} %get-tuple-element.135, ...), kind=kOutput, calls=%fused_computation.2.clone.1 | convolution fusion | flops 1612972032 | bytes 8914944 | tf_op jit(solution)/shard_map/while/body/eval_jaxpr/vsac,dc->vsad/dot_general | solution.py:18
  154.4 5.7 %fusion.25 = f32[3,8,512,512]{3,2,1,0:T(8,128)} fusion(f32[3,8,512,512]{3,2,1,0:T(8,128)} %get-tuple-element.122, s32[]{:T(128)} %bitcast.60, f32[3,1,512,512]{3,2,1,0:T(8,128)S(1)} %constant_dynamic-slice_fusion.6, pred[]{:T(512)} %and_reduce_fusion.2, bf16[3,1,512,512]{3,2,0,1:T(8,128)(2,1)} %get-tuple-element.135, ...), kind=kOutput, calls=%fused_computation.2.clone.1 | convolution fusion | flops 1612972032 | bytes 8914944 | tf_op jit(solution)/shard_map/while/body/eval_jaxpr/vsac,dc->vsad/dot_general | solution.py:18
  165.3 5.8 %fusion.25 = f32[3,8,512,512]{3,2,1,0:T(8,128)} fusion(f32[3,8,512,512]{3,2,1,0:T(8,128)} %get-tuple-element.122, s32[]{:T(128)} %bitcast.60, f32[3,1,512,512]{3,2,1,0:T(8,128)S(1)} %constant_dynamic-slice_fusion.6, pred[]{:T(512)} %and_reduce_fusion.2, bf16[3,1,512,512]{3,2,0,1:T(8,128)(2,1)} %get-tuple-element.135, ...), kind=kOutput, calls=%fused_computation.2.clone.1 | convolution fusion | flops 1612972032 | bytes 8914944 | tf_op jit(solution)/shard_map/while/body/eval_jaxpr/vsac,dc->vsad/dot_general | solution.py:18
  176.2 5.7 %fusion.25 = f32[3,8,512,512]{3,2,1,0:T(8,128)} fusion(f32[3,8,512,512]{3,2,1,0:T(8,128)} %get-tuple-element.122, s32[]{:T(128)} %bitcast.60, f32[3,1,512,512]{3,2,1,0:T(8,128)S(1)} %constant_dynamic-slice_fusion.6, pred[]{:T(512)} %and_reduce_fusion.2, bf16[3,1,512,512]{3,2,0,1:T(8,128)(2,1)} %get-tuple-element.135, ...), kind=kOutput, calls=%fused_computation.2.clone.1 | convolution fusion | flops 1612972032 | bytes 8914944 | tf_op jit(solution)/shard_map/while/body/eval_jaxpr/vsac,dc->vsad/dot_general | solution.py:18
  187.1 5.8 %fusion.25 = f32[3,8,512,512]{3,2,1,0:T(8,128)} fusion(f32[3,8,512,512]{3,2,1,0:T(8,128)} %get-tuple-element.122, s32[]{:T(128)} %bitcast.60, f32[3,1,512,512]{3,2,1,0:T(8,128)S(1)} %constant_dynamic-slice_fusion.6, pred[]{:T(512)} %and_reduce_fusion.2, bf16[3,1,512,512]{3,2,0,1:T(8,128)(2,1)} %get-tuple-element.135, ...), kind=kOutput, calls=%fused_computation.2.clone.1 | convolution fusion | flops 1612972032 | bytes 8914944 | tf_op jit(solution)/shard_map/while/body/eval_jaxpr/vsac,dc->vsad/dot_general | solution.py:18
  194.1 142.8 %reduce-scatter.5.cloned.1.call-done = f32[3,8,32,512]{3,2,1,0:T(8,128)} async-done(((f32[3,8,512,512]{3,2,1,0:T(8,128)}), f32[3,8,32,512]{3,2,1,0:T(8,128)}) %reduce-scatter.5.cloned.1.call-update) | async-done | bytes 1572880 | tf_op jit(solution)/shard_map/reduce_scatter | solution.py:25
  336.9 81.9 %all-reduce.2 = bf16[3,8,32,512]{3,2,1,0:T(8,128)(2,1)S(1)} all-reduce(f32[3,8,32,512]{3,2,1,0:T(8,128)} %reduce-scatter.5.cloned.1.call-done), channel_id=3, replica_groups=mesh['op'=16,'sec'=8] {'sec'}, use_global_device_ids=true, to_apply=%region_4.5.clone | all-reduce | flops 393216 | bytes 2359296
  (55 shorter events, 49.9 us)
Async XLA Ops:
  6.5 0.7 copy-start
  6.5 330.4 %reduce-scatter.5.cloned.1.call-start = ((), (), s32[]{:S(2)}) async-start(), calls=%async_computation.1 | async-start | bytes 26738688 | tf_op jit(solution)/shard_map/reduce_scatter | solution.py:25
  7.2 11.5 %copy-start.1 = (s32[4]{0:T(128)S(1)}, s32[4]{0:T(128)}, u32[]{:S(2)}) copy-start(s32[4]{0:T(128)} %constant.39.clone.1) | copy-start | bytes 52
  192.9 0.7 copy-start.2
Sparse Core Ops, SparseCore 0:
  193.0 143.8 reduce-scatter.4
where the time goes:
time: 429 us; the launch traced here: 427 us
  waiting for transfers between devices  143 us (33%)
  matrix products  91.6 us (21%)
  blocking collectives  81.9 us (19%)
  local copies, waits for them, and re-layouts  59 us (14%)
  loops' own time  27 us (6%)
  between operations  13.4 us (3%)
  other arithmetic  11.3 us (3%)
    reduce_scatter x1, waiting for transfers between devices, per_device(): lax.psum_scatter(partial_sums, 'op', scatter_dimension=2, tiled=True)  143 us
    dot_general x16, matrix products, source_operator(): jnp.einsum('vsac,dc->vsad', middle, right_block, preferred_element_type=j...  91.6 us
    unnamed x1, blocking collectives  81.9 us
    another operation x16, local copies, waits for them, and re-layouts  35.1 us
    another operation x1, loops' own time, per_device(): lax.scan(source_operator, start_value, (left_ops, right_ops, owned_ids))  27 us
    broadcast_in_dim x1, local copies, waits for them, and re-layouts, per_device(): jnp.zeros((vectors, sec_total, block_size, block_size), jnp.float32)  11.5 us
    another operation x16, other arithmetic  11.3 us
    dynamic_slice x16, local copies, waits for them, and re-layouts, per_device(): lax.scan(source_operator, start_value, (left_ops, right_ops, owned_ids))  9.17 us
  transfers between devices with their start and end apart: 1, of which 1 were waited for; matrix products, arithmetic and copies ran while one was open for 0% of the time, Pallas kernels for 0%

commit v1 on v0

v1 whole, which is shorter than its diff:
```python
import functools

import jax
import jax.numpy as jnp
from jax import lax
from jax.experimental import pallas as pl
from jax.experimental.pallas import tpu as pltpu
from jax.sharding import PartitionSpec as P

F32 = jnp.float32
BF16 = jnp.bfloat16
MESH = pl.DeviceIdType.MESH
UNROLL = 4
HALF = 2


def kernel(psi_hbm, left_hbm, right_hbm, targets, out_ref, *scratch):
    vectors = psi_hbm.shape[0]
    ops, size, _ = left_hbm.shape
    sectors = targets.shape[1]
    chunks = vectors * HALF
    width = size // HALF
    rows_core = size // 2
    shard = rows_core // 4
    peers = 16
    rows_out = size // peers

    bufs = scratch[:chunks]
    (left, right, acc, own, sbuf, rbuf, s1_send, s1_recv, sh_send, sh_recv, mt_send, mt_recv,
     rs_send, rs_recv, load_sem, own_sem) = scratch[chunks:]

    op = lax.axis_index("op")
    sec = lax.axis_index("sec")
    core = lax.rem(op, 2)
    y = lax.rem(op // 2, 4)
    zl = op // 8
    x = lax.rem(sec, 4)
    zh = sec // 4

    def op_of(zl_, y_, core_):
        return zl_ * 8 + y_ * 2 + core_

    routes = ((2, 1, 7), (2, 0, 4), (1, 1, 6), (3, 1, 5), (1, 0, 2), (3, 0, 1), (0, 1, 3))

    def sec_peer(dx, dz):
        x_ = lax.rem(x + dx, 4)
        if dz:
            return op_of(1 - zl, y, core), (1 - zh) * 4 + x_
        return op, zh * 4 + x_

    near = (op_of(zl, lax.rem(y + 1, 4), core), op_of(zl, lax.rem(y + 3, 4), core), op_of(1 - zl, y, core))
    mate = op_of(zl, y, 1 - core)
    colour = lax.rem(y + 2 * zl, 4)
    base = core * rows_core

    def shard_rows(q):
        return pl.ds(pl.multiple_of(base + q * shard, 16), shard)

    barrier = pltpu.get_barrier_semaphore()
    for dx, dz, _ in routes:
        pl.semaphore_signal(barrier, inc=1, device_id=sec_peer(dx, dz), device_id_type=MESH)
    for j in range(1, peers):
        pl.semaphore_signal(barrier, inc=1, device_id=(lax.rem(op + j, peers), sec), device_id_type=MESH)
    own_copies = []
    for ch in range(chunks):
        v, h = divmod(ch, HALF)
        own_copies.append(pltpu.make_async_copy(
            psi_hbm.at[v, 0, :, h * width:(h + 1) * width], bufs[ch].at[0], own_sem.at[ch]))
        own_copies[-1].start()
    loads = [pltpu.make_async_copy(left_hbm, left, load_sem.at[0]),
             pltpu.make_async_copy(right_hbm, right, load_sem.at[1])]
    pl.semaphore_wait(barrier, len(routes) + peers - 1)

    first = []
    for ch in range(chunks):
        v, h = divmod(ch, HALF)
        for i, (dx, dz, slot) in enumerate(routes):
            rows = shard_rows(lax.rem(colour + 2 * dz, 4))
            first.append(pltpu.make_async_remote_copy(
                src_ref=psi_hbm.at[v, 0, rows, h * width:(h + 1) * width],
                dst_ref=bufs[ch].at[slot, rows, :],
                send_sem=s1_send.at[ch, i], recv_sem=s1_recv.at[ch, i],
                device_id=sec_peer(dx, dz), device_id_type=MESH))
    share = []
    for ch in range(chunks):
        rows = shard_rows(colour)
        for i in range(3):
            share.append(pltpu.make_async_remote_copy(
                src_ref=bufs[ch].at[1:8, rows, :], dst_ref=bufs[ch].at[1:8, rows, :],
                send_sem=sh_send.at[ch, i], recv_sem=sh_recv.at[ch, i],
                device_id=(near[i], sec), device_id_type=MESH))
    cross = []
    for ch in range(chunks):
        rows = pl.ds(pl.multiple_of(base, rows_core), rows_core)
        cross.append(pltpu.make_async_remote_copy(
            src_ref=bufs[ch].at[1:8, rows, :], dst_ref=bufs[ch].at[1:8, rows, :],
            send_sem=mt_send.at[ch], recv_sem=mt_recv.at[ch],
            device_id=(mate, sec), device_id_type=MESH))

    for copy in first[:len(routes)]:
        copy.start()
    for copy in loads:
        copy.start()
    for copy in first[len(routes):]:
        copy.start()

    def step_share(ch):
        for copy in first[ch * 7:ch * 7 + 7]:
            copy.wait_recv()
        for copy in share[ch * 3:ch * 3 + 3]:
            copy.start()

    def step_cross(ch):
        for copy in share[ch * 3:ch * 3 + 3]:
            copy.wait_recv()
        cross[ch].start()

    def step_ready(ch):
        cross[ch].wait_recv()
        own_copies[ch].wait()

    def slot_of(k):
        source = jnp.int32(0)
        for s in range(sectors):
            source = source + jnp.where(targets[k, s] == sec, s, 0)
        d = lax.rem(lax.rem(source, 4) - x + 4, 4)
        same = source // 4 == zh
        return jnp.where(same, jnp.where(d == 0, 0, jnp.where(d == 1, 1, jnp.where(d == 3, 2, 4))),
                         jnp.where(d == 0, 3, jnp.where(d == 1, 5, jnp.where(d == 3, 6, 7))))

    def compute(ch, start, stop):
        h = ch % HALF
        cols = slice(h * width, (h + 1) * width)

        def body(i, carry):
            mids = []
            for u in range(UNROLL):
                k = i * UNROLL + u
                mids.append(jnp.dot(left[k], bufs[ch][slot_of(k)], preferred_element_type=F32).astype(BF16))
            total = None
            for u in range(UNROLL):
                part = lax.dot_general(mids[u], right[i * UNROLL + u, :, cols], (((1,), (1,)), ((), ())),
                                       preferred_element_type=F32)
                total = part if total is None else total + part
            acc[...] += total
            return carry

        lax.fori_loop(start // UNROLL, stop // UNROLL, body, 0)

    def reduce_copies(v):
        copies = []
        for j in range(1, peers):
            to = lax.rem(op + j, peers)
            copies.append(pltpu.make_async_remote_copy(
                src_ref=sbuf.at[v, pl.ds(pl.multiple_of(to * rows_out, rows_out), rows_out), :],
                dst_ref=rbuf.at[v, j - 1],
                send_sem=rs_send.at[v, j - 1], recv_sem=rs_recv.at[v, j - 1],
                device_id=(to, sec), device_id_type=MESH))
        return copies

    reduces = []
    step_share(0)
    step_share(1)
    step_cross(0)
    for copy in loads:
        copy.wait()
    for ch in range(chunks):
        v, h = divmod(ch, HALF)
        step_ready(ch)
        if h == 0:
            acc[...] = jnp.zeros_like(acc)
        compute(ch, 0, ops // 2)
        if ch + 1 < chunks:
            step_cross(ch + 1)
        compute(ch, ops // 2, ops)
        if ch + 2 < chunks:
            step_share(ch + 2)
        if h == HALF - 1:
            sbuf[v] = acc[...].astype(BF16)
            own[v] = acc[pl.ds(pl.multiple_of(op * rows_out, rows_out), rows_out), :]
            reduces.append(reduce_copies(v))
            for copy in reduces[v]:
                copy.start()

    for v in range(vectors):
        for copy in reduces[v]:
            copy.wait_recv()
        total = own[v]
        for j in range(peers - 1):
            total = total + rbuf[v, j].astype(F32)
        out_ref[v, 0] = total.astype(BF16)

    for copy in first + share + cross:
        copy.wait_send()
    for copies in reduces:
        for copy in copies:
            copy.wait_send()


def per_device(wavefunction, left_ops, right_ops, targets):
    vectors, _, size, _ = wavefunction.shape
    ops = left_ops.shape[0]
    chunks = vectors * HALF
    width = size // HALF
    dma = pltpu.SemaphoreType.DMA
    scratch = [pltpu.VMEM((8, size, width), BF16) for _ in range(chunks)] + [
        pltpu.VMEM((ops, size, size), BF16),
        pltpu.VMEM((ops, size, size), BF16),
        pltpu.VMEM((size, size), F32),
        pltpu.VMEM((vectors, size // 16, size), F32),
        pltpu.VMEM((vectors, size, size), BF16),
        pltpu.VMEM((vectors, 15, size // 16, size), BF16),
        dma((chunks, 7)), dma((chunks, 7)), dma((chunks, 3)), dma((chunks, 3)), dma((chunks,)), dma((chunks,)),
        dma((vectors, 15)), dma((vectors, 15)), dma((2,)), dma((chunks,)),
    ]
    hbm = pl.BlockSpec(memory_space=pl.ANY)
    return pl.pallas_call(
        kernel,
        out_shape=jax.ShapeDtypeStruct((vectors, 1, size // 16, size), BF16),
        in_specs=[hbm, hbm, hbm, pl.BlockSpec(memory_space=pltpu.SMEM)],
        out_specs=pl.BlockSpec(memory_space=pltpu.VMEM),
        scratch_shapes=scratch,
        compiler_params=pltpu.CompilerParams(
            collective_id=0, has_side_effects=True, vmem_limit_bytes=62 * 2**20),
        name="sigma",
    )(wavefunction, left_ops, right_ops, targets)


def solution(mesh):
    return jax.shard_map(
        per_device,
        mesh=mesh,
        in_specs=(
            P(None, "sec", None, None),
            P("op", None, None),
            P("op", None, None),
            P("op", None),
        ),
        out_specs=P(None, "sec", "op", None),
        check_vma=False,
    )
```

time: 429 us -> 91 us (0.21)
  waiting for transfers between devices: 143 us -> 0 us
  matrix products: 91.6 us -> 0 us
  Pallas kernels: 0 us -> 87.3 us
  blocking collectives: 81.9 us -> 0 us
  local copies, waits for them, and re-layouts: 59 us -> 2.89 us
  loops' own time: 27 us -> 0 us
  between operations: 13.4 us -> 0.01 us
  other arithmetic: 11.3 us -> 0 us
    reduce_scatter x1 -> x0, waiting for transfers between devices: 143 us -> none  [per_device(): lax.psum_scatter(partial_sums, 'op', scatter_dimension=2, tiled=True)]
    dot_general x16 -> x0, matrix products: 91.6 us -> none  [source_operator(): jnp.einsum('vsac,dc->vsad', middle, right_block, preferred_element_type=j...]
    pallas_call x0 -> x1, Pallas kernels: none -> 87.3 us  [per_device(): pl.pallas_call(kernel, out_shape=jax.ShapeDtypeStruct((vectors, 1, size /...]
    unnamed x1 -> x0, blocking collectives: 81.9 us -> none
    another operation x16 -> x0, local copies, waits for them, and re-layouts: 35.1 us -> none
    another operation x1 -> x0, loops' own time: 27 us -> none  [per_device(): lax.scan(source_operator, start_value, (left_ops, right_ops, owned_ids))]
    broadcast_in_dim x1 -> x0, local copies, waits for them, and re-layouts: 11.5 us -> none  [per_device(): jnp.zeros((vectors, sec_total, block_size, block_size), jnp.float32)]
    another operation x16 -> x0, other arithmetic: 11.3 us -> none
  transfers between devices with their start and end apart: 1 -> 0, of which waited for: 1 -> 0; matrix products, arithmetic and copies ran while one was open for 0% -> 0% of each run, Pallas kernels for 0% -> 0%
where the time goes in v1:
time: 91 us; the launch traced here: 90.2 us
  Pallas kernels  87.3 us (96%)
  local copies, waits for them, and re-layouts  2.89 us (3%)
    pallas_call x1, Pallas kernels, per_device(): pl.pallas_call(kernel, out_shape=jax.ShapeDtypeStruct((vectors, 1, size /...  87.3 us
    unnamed x2, local copies, waits for them, and re-layouts  2.89 us

profile of v1, /device:TPU:0, one launch (start us, length us, event | category | flops | bytes accessed | tf_op | source)
XLA Modules:
  0.0 90.2 jit_solution(1335045447205988693)
XLA Ops:
  0.0 1.4 %copy.5.targets = s32[16,8]{1,0:T(8,128)} copy(s32[16,8]{0,1:T(8,128)} %param.7) | data formatting | bytes 1024 | tf_op args[3]
  1.4 87.3 %sigma.1 = bf16[3,1,32,512]{3,2,1,0:T(8,128)(2,1)} custom-call(bf16[3,1,512,512]{3,2,1,0:T(8,128)(2,1)} %psi_hbm.1, bf16[16,512,512]{2,1,0:T(8,128)(2,1)} %left_hbm.1, bf16[16,512,512]{2,1,0:T(8,128)(2,1)} %right_hbm.1, s32[16,8]{1,0:T(8,128)} %copy.5.targets), custom_call_target="tpu_custom_call" | custom-call | tf_op jit(solution)/shard_map/sigma/pallas_call | solution.py:217
  88.7 1.5 %copy.7 = bf16[3,1,32,512]{3,2,1,0:T(8,128)(2,1)} copy(bf16[3,1,32,512]{3,2,1,0:T(8,128)(2,1)} %sigma.1) | data formatting | bytes 196608

commit v2 on v1

v2 whole, which is shorter than its diff:
```python
import jax
import jax.numpy as jnp
from jax import lax
from jax.experimental import pallas as pl
from jax.experimental.pallas import tpu as pltpu
from jax.sharding import PartitionSpec as P

F32 = jnp.float32
BF16 = jnp.bfloat16
MESH = pl.DeviceIdType.MESH
UNROLL = 4
HALF = 2
UNITS = 3


def kernel(psi_hbm, left_hbm, right_hbm, targets, out_ref, *scratch):
    vectors = psi_hbm.shape[0]
    ops, size, _ = left_hbm.shape
    sectors = targets.shape[1]
    width = size // HALF
    rows_core = size // 2
    shard = rows_core // 4
    peers = 16
    rows_out = size // peers
    chunks = 2 * HALF

    bufs = scratch[:chunks]
    (left, right, acc, sbuf, rbuf, s1_send, s1_recv, sh_send, sh_recv, mt_send, mt_recv,
     rs_send, rs_recv, load_sem, own_sem, self_sem) = scratch[chunks:]

    op = lax.axis_index("op")
    sec = lax.axis_index("sec")
    core = lax.rem(op, 2)
    y = lax.rem(op // 2, 4)
    zl = op // 8
    x = lax.rem(sec, 4)
    zh = sec // 4

    def op_of(zl_, y_, core_):
        return zl_ * 8 + y_ * 2 + core_

    def vector_a(d):
        return (3 * d + 1) // sectors

    def two_vectors(d):
        return jnp.logical_or(d == 2, d == 5)

    both = two_vectors(sec)
    units = (3 * sec + 1, jnp.where(sec == 5, 3 * sec + 2, 3 * sec), jnp.where(sec == 5, 3 * sec, 3 * sec + 2))
    unit_vector = [u // sectors for u in units]
    unit_target = [lax.rem(u, sectors) for u in units]

    routes = ((2, 1, 7), (2, 0, 4), (1, 1, 6), (3, 1, 5), (1, 0, 2), (3, 0, 1), (0, 1, 3))

    def sec_peer(dx, dz):
        x_ = lax.rem(x + dx, 4)
        if dz:
            return op_of(1 - zl, y, core), (1 - zh) * 4 + x_
        return op, zh * 4 + x_

    near = (op_of(zl, lax.rem(y + 1, 4), core), op_of(zl, lax.rem(y + 3, 4), core), op_of(1 - zl, y, core))
    mate = op_of(zl, y, 1 - core)
    colour = lax.rem(y + 2 * zl, 4)
    base = core * rows_core

    def shard_rows(q):
        return pl.ds(pl.multiple_of(base + q * shard, 16), shard)

    barrier = pltpu.get_barrier_semaphore()
    for dx, dz, _ in routes:
        pl.semaphore_signal(barrier, inc=1, device_id=sec_peer(dx, dz), device_id_type=MESH)
    for j in range(1, peers):
        pl.semaphore_signal(barrier, inc=1, device_id=(lax.rem(op + j, peers), sec), device_id_type=MESH)

    own_copies, first, share, cross = [], [], [], []
    for ch in range(chunks):
        is_b, h = divmod(ch, HALF)
        cols = slice(h * width, (h + 1) * width)
        own_copies.append(pltpu.make_async_copy(
            psi_hbm.at[1 if is_b else vector_a(sec), 0, :, cols], bufs[ch].at[0], own_sem.at[ch]))
        copies = []
        for i, (dx, dz, slot) in enumerate(routes):
            rows = shard_rows(lax.rem(colour + 2 * dz, 4))
            peer = sec_peer(dx, dz)
            copies.append((two_vectors(peer[1]) if is_b else None, pltpu.make_async_remote_copy(
                src_ref=psi_hbm.at[1 if is_b else vector_a(peer[1]), 0, rows, cols],
                dst_ref=bufs[ch].at[slot, rows, :],
                send_sem=s1_send.at[ch, i], recv_sem=s1_recv.at[ch, i],
                device_id=peer, device_id_type=MESH)))
        first.append(copies)
        rows = shard_rows(colour)
        share.append([pltpu.make_async_remote_copy(
            src_ref=bufs[ch].at[1:8, rows, :], dst_ref=bufs[ch].at[1:8, rows, :],
            send_sem=sh_send.at[ch, i], recv_sem=sh_recv.at[ch, i],
            device_id=(near[i], sec), device_id_type=MESH) for i in range(3)])
        rows = pl.ds(pl.multiple_of(base, rows_core), rows_core)
        cross.append(pltpu.make_async_remote_copy(
            src_ref=bufs[ch].at[1:8, rows, :], dst_ref=bufs[ch].at[1:8, rows, :],
            send_sem=mt_send.at[ch], recv_sem=mt_recv.at[ch],
            device_id=(mate, sec), device_id_type=MESH))
    loads = [pltpu.make_async_copy(left_hbm, left, load_sem.at[0]),
             pltpu.make_async_copy(right_hbm, right, load_sem.at[1])]

    def when(condition, action):
        if condition is None:
            action()
        else:
            pl.when(condition)(action)

    def start_first(ch):
        for condition, copy in first[ch]:
            when(condition, copy.start)

    def step_share(ch):
        for _, copy in first[ch]:
            copy.wait_recv()
        for copy in share[ch]:
            copy.start()

    def step_cross(ch):
        for copy in share[ch]:
            copy.wait_recv()
        cross[ch].start()

    def step_ready(ch):
        cross[ch].wait_recv()
        own_copies[ch].wait()

    own_copies[0].start()
    own_copies[1].start()
    for copy in loads:
        copy.start()
    pl.semaphore_wait(barrier, len(routes) + peers - 1)
    for ch in range(chunks):
        start_first(ch)

    @pl.when(both)
    def _():
        own_copies[2].start()
        own_copies[3].start()

    def slot_of(k, target):
        source = jnp.int32(0)
        for s in range(sectors):
            source = source + jnp.where(targets[k, s] == target, s, 0)
        d = lax.rem(lax.rem(source, 4) - x + 4, 4)
        same = source // 4 == zh
        return jnp.where(same, jnp.where(d == 0, 0, jnp.where(d == 1, 1, jnp.where(d == 3, 2, 4))),
                         jnp.where(d == 0, 3, jnp.where(d == 1, 5, jnp.where(d == 3, 6, 7))))

    def compute(unit, ch):
        h = ch % HALF
        cols = slice(h * width, (h + 1) * width)
        at = unit % 2

        def body(i, carry):
            mids = []
            for u in range(UNROLL):
                k = i * UNROLL + u
                mids.append(jnp.dot(left[k], bufs[ch][slot_of(k, unit_target[unit])],
                                    preferred_element_type=F32).astype(BF16))
            total = None
            for u in range(UNROLL):
                part = lax.dot_general(mids[u], right[i * UNROLL + u, :, cols], (((1,), (1,)), ((), ())),
                                       preferred_element_type=F32)
                total = part if total is None else total + part
            acc[at] += total
            return carry

        if h == 0:
            acc[at] = jnp.zeros((size, size), F32)
        lax.fori_loop(0, ops // UNROLL, body, 0)

    def out_rows(to):
        return pl.ds(pl.multiple_of(to * rows_out, rows_out), rows_out)

    def reduce_copy(unit, j):
        to = lax.rem(op + j, peers)
        return pltpu.make_async_remote_copy(
            src_ref=sbuf.at[unit, out_rows(to), :],
            dst_ref=rbuf.at[unit_vector[unit], op],
            send_sem=rs_send.at[unit, j], recv_sem=rs_recv.at[unit_vector[unit], op],
            device_id=(to, unit_target[unit]), device_id_type=MESH)

    def keep_copy(unit):
        return pltpu.make_async_copy(sbuf.at[unit, out_rows(op), :], rbuf.at[unit_vector[unit], op], self_sem.at[0])

    def send(unit):
        sbuf[unit] = acc[unit % 2].astype(BF16)
        for j in range(1, peers):
            reduce_copy(unit, j).start()
        mine = unit_target[unit] == sec
        pl.when(jnp.logical_not(mine))(lambda: reduce_copy(unit, 0).start())
        pl.when(mine)(lambda: keep_copy(unit).start())

    step_share(0)
    step_share(1)
    step_cross(0)
    for copy in loads:
        copy.wait()
    step_ready(0)
    compute(0, 0)
    step_cross(1)

    @pl.when(both)
    def _():
        step_share(2)
        step_share(3)

    compute(1, 0)
    step_ready(1)
    compute(0, 1)
    send(0)
    pl.when(both)(lambda: step_cross(2))
    compute(1, 1)
    send(1)

    @pl.when(both)
    def _():
        step_cross(3)
        step_ready(2)
        compute(2, 2)
        step_ready(3)
        compute(2, 3)

    @pl.when(jnp.logical_not(both))
    def _():
        compute(2, 0)
        compute(2, 1)

    send(2)

    for unit in range(UNITS):
        pl.when(unit_target[unit] == sec)(lambda: keep_copy(unit).wait())
    for v in range(vectors):
        def arrival(j):
            source = lax.rem(op + j, peers)
            return pltpu.make_async_remote_copy(
                src_ref=sbuf.at[0, out_rows(op), :], dst_ref=rbuf.at[v, source],
                send_sem=rs_send.at[0, j], recv_sem=rs_recv.at[v, source],
                device_id=(source, sec), device_id_type=MESH)

        pl.when((sectors * v + sec) // UNITS != sec)(lambda: arrival(0).wait_recv())
        for j in range(1, peers):
            arrival(j).wait_recv()
        total = rbuf[v, 0].astype(F32)
        for j in range(1, peers):
            total = total + rbuf[v, j].astype(F32)
        out_ref[v, 0] = total.astype(BF16)

    for ch in range(chunks):
        for condition, copy in first[ch]:
            when(condition, copy.wait_send)

        def sent():
            for copy in share[ch] + [cross[ch]]:
                copy.wait_send()

        when(both if ch >= HALF else None, sent)
    for unit in range(UNITS):
        for j in range(1, peers):
            reduce_copy(unit, j).wait_send()
        pl.when(unit_target[unit] != sec)(lambda: reduce_copy(unit, 0).wait_send())


def per_device(wavefunction, left_ops, right_ops, targets):
    vectors, _, size, _ = wavefunction.shape
    ops = left_ops.shape[0]
    chunks = 2 * HALF
    width = size // HALF
    dma = pltpu.SemaphoreType.DMA
    scratch = [pltpu.VMEM((8, size, width), BF16) for _ in range(chunks)] + [
        pltpu.VMEM((ops, size, size), BF16),
        pltpu.VMEM((ops, size, size), BF16),
        pltpu.VMEM((2, size, size), F32),
        pltpu.VMEM((UNITS, size, size), BF16),
        pltpu.VMEM((vectors, 16, size // 16, size), BF16),
        dma((chunks, 7)), dma((chunks, 7)), dma((chunks, 3)), dma((chunks, 3)), dma((chunks,)), dma((chunks,)),
        dma((UNITS, 16)), dma((vectors, 16)), dma((2,)), dma((chunks,)), dma((1,)),
    ]
    hbm = pl.BlockSpec(memory_space=pl.ANY)
    return pl.pallas_call(
        kernel,
        out_shape=jax.ShapeDtypeStruct((vectors, 1, size // 16, size), BF16),
        in_specs=[hbm, hbm, hbm, pl.BlockSpec(memory_space=pltpu.SMEM)],
        out_specs=pl.BlockSpec(memory_space=pltpu.VMEM),
        scratch_shapes=scratch,
        compiler_params=pltpu.CompilerParams(
            collective_id=0, has_side_effects=True, vmem_limit_bytes=62 * 2**20),
        name="sigma",
    )(wavefunction, left_ops, right_ops, targets)


def solution(mesh):
    return jax.shard_map(
        per_device,
        mesh=mesh,
        in_specs=(
            P(None, "sec", None, None),
            P("op", None, None),
            P("op", None, None),
            P("op", None),
        ),
        out_specs=P(None, "sec", "op", None),
        check_vma=False,
    )
```

time: 91 us -> 75.1 us (0.83)
  Pallas kernels: 87.3 us -> 70.9 us
    pallas_call x1, Pallas kernels: 87.3 us -> 70.9 us  [per_device(): pl.pallas_call(kernel, out_shape=jax.ShapeDtypeStruct((vectors, 1, size /...]
where the time goes in v2:
time: 75.1 us; the launch traced here: 73.8 us
  Pallas kernels  70.9 us (94%)
  local copies, waits for them, and re-layouts  2.89 us (4%)
    pallas_call x1, Pallas kernels, per_device(): pl.pallas_call(kernel, out_shape=jax.ShapeDtypeStruct((vectors, 1, size /...  70.9 us
    unnamed x2, local copies, waits for them, and re-layouts  2.89 us

profile of v2, /device:TPU:0, one launch (start us, length us, event | category | flops | bytes accessed | tf_op | source)
XLA Modules:
  0.0 73.8 jit_solution(17243930189431050744)
XLA Ops:
  0.0 1.4 %copy.5.targets = s32[16,8]{1,0:T(8,128)} copy(s32[16,8]{0,1:T(8,128)} %param.7) | data formatting | bytes 1024 | tf_op args[3]
  1.4 70.9 %sigma.1 = bf16[3,1,32,512]{3,2,1,0:T(8,128)(2,1)} custom-call(bf16[3,1,512,512]{3,2,1,0:T(8,128)(2,1)} %psi_hbm.1, bf16[16,512,512]{2,1,0:T(8,128)(2,1)} %left_hbm.1, bf16[16,512,512]{2,1,0:T(8,128)(2,1)} %right_hbm.1, s32[16,8]{1,0:T(8,128)} %copy.5.targets), custom_call_target="tpu_custom_call" | custom-call | tf_op jit(solution)/shard_map/sigma/pallas_call | solution.py:282
  72.2 1.5 %copy.7 = bf16[3,1,32,512]{3,2,1,0:T(8,128)(2,1)} copy(bf16[3,1,32,512]{3,2,1,0:T(8,128)(2,1)} %sigma.1) | data formatting | bytes 196608

commit v3 on v2

--- a/solution.py
+++ b/solution.py
@@ -21,12 +21,13 @@
     rows_core = size // 2
     shard = rows_core // 4
     peers = 16
+    chips = peers // 2
     rows_out = size // peers
     chunks = 2 * HALF
 
     bufs = scratch[:chunks]
-    (left, right, acc, sbuf, rbuf, s1_send, s1_recv, sh_send, sh_recv, mt_send, mt_recv,
-     rs_send, rs_recv, load_sem, own_sem, self_sem) = scratch[chunks:]
+    (left, right, acc, sbuf, mbuf, tbuf, rbuf, s1_send, s1_recv, sh_send, sh_recv, mt_send, mt_recv,
+     pr_send, pr_recv, rs_send, rs_recv, load_sem, own_sem, self_sem) = scratch[chunks:]
 
     op = lax.axis_index("op")
     sec = lax.axis_index("sec")
@@ -148,10 +149,10 @@
         return jnp.where(same, jnp.where(d == 0, 0, jnp.where(d == 1, 1, jnp.where(d == 3, 2, 4))),
                          jnp.where(d == 0, 3, jnp.where(d == 1, 5, jnp.where(d == 3, 6, 7))))
 
-    def compute(unit, ch):
+    def compute(unit, ch, start=0, stop=None):
         h = ch % HALF
         cols = slice(h * width, (h + 1) * width)
-        at = unit % 2
+        at = unit
 
         def body(i, carry):
             mids = []
@@ -164,30 +165,40 @@
                 part = lax.dot_general(mids[u], right[i * UNROLL + u, :, cols], (((1,), (1,)), ((), ())),
                                        preferred_element_type=F32)
                 total = part if total is None else total + part
-            acc[at] += total
+            acc[at] += total.reshape(chips, 2, rows_out, size)
             return carry
 
-        if h == 0:
-            acc[at] = jnp.zeros((size, size), F32)
-        lax.fori_loop(0, ops // UNROLL, body, 0)
-
-    def out_rows(to):
-        return pl.ds(pl.multiple_of(to * rows_out, rows_out), rows_out)
+        if h == 0 and start == 0:
+            acc[at] = jnp.zeros(acc.shape[1:], F32)
+        lax.fori_loop(start // UNROLL, (ops if stop is None else stop) // UNROLL, body, 0)
+
+    chip = op // 2
+
+    def pair_copy(unit):
+        return pltpu.make_async_remote_copy(
+            src_ref=sbuf.at[unit], dst_ref=mbuf.at[unit],
+            send_sem=pr_send.at[unit], recv_sem=pr_recv.at[unit],
+            device_id=(mate, sec), device_id_type=MESH)
 
     def reduce_copy(unit, j):
-        to = lax.rem(op + j, peers)
+        to = lax.rem(chip + j, chips)
         return pltpu.make_async_remote_copy(
-            src_ref=sbuf.at[unit, out_rows(to), :],
-            dst_ref=rbuf.at[unit_vector[unit], op],
-            send_sem=rs_send.at[unit, j], recv_sem=rs_recv.at[unit_vector[unit], op],
-            device_id=(to, unit_target[unit]), device_id_type=MESH)
+            src_ref=tbuf.at[unit, to],
+            dst_ref=rbuf.at[unit_vector[unit], chip],
+            send_sem=rs_send.at[unit, j], recv_sem=rs_recv.at[unit_vector[unit], chip],
+            device_id=(2 * to + core, unit_target[unit]), device_id_type=MESH)
 
     def keep_copy(unit):
-        return pltpu.make_async_copy(sbuf.at[unit, out_rows(op), :], rbuf.at[unit_vector[unit], op], self_sem.at[0])
+        return pltpu.make_async_copy(tbuf.at[unit, chip], rbuf.at[unit_vector[unit], chip], self_sem.at[0])
+
+    def send_pair(unit):
+        sbuf[unit] = acc[unit, :, 1 - core].astype(BF16)
+        pair_copy(unit).start()
 
     def send(unit):
-        sbuf[unit] = acc[unit % 2].astype(BF16)
-        for j in range(1, peers):
+        pair_copy(unit).wait_recv()
+        tbuf[unit] = (acc[unit, :, core] + mbuf[unit].astype(F32)).astype(BF16)
+        for j in (4, 5, 3, 6, 2, 7, 1):
             reduce_copy(unit, j).start()
         mine = unit_target[unit] == sec
         pl.when(jnp.logical_not(mine))(lambda: reduce_copy(unit, 0).start())
@@ -210,41 +221,46 @@
     compute(1, 0)
     step_ready(1)
     compute(0, 1)
+    send_pair(0)
+    pl.when(both)(lambda: step_cross(2))
+    compute(1, 1, 0, ops // 2)
     send(0)
-    pl.when(both)(lambda: step_cross(2))
-    compute(1, 1)
-    send(1)
+    compute(1, 1, ops // 2)
+    send_pair(1)
 
     @pl.when(both)
     def _():
         step_cross(3)
         step_ready(2)
         compute(2, 2)
+        send(1)
         step_ready(3)
         compute(2, 3)
 
     @pl.when(jnp.logical_not(both))
     def _():
         compute(2, 0)
+        send(1)
         compute(2, 1)
 
+    send_pair(2)
     send(2)
 
     for unit in range(UNITS):
         pl.when(unit_target[unit] == sec)(lambda: keep_copy(unit).wait())
     for v in range(vectors):
         def arrival(j):
-            source = lax.rem(op + j, peers)
+            source = lax.rem(chip + j, chips)
             return pltpu.make_async_remote_copy(
-                src_ref=sbuf.at[0, out_rows(op), :], dst_ref=rbuf.at[v, source],
+                src_ref=tbuf.at[0, chip], dst_ref=rbuf.at[v, source],
                 send_sem=rs_send.at[0, j], recv_sem=rs_recv.at[v, source],
-                device_id=(source, sec), device_id_type=MESH)
+                device_id=(2 * source + core, sec), device_id_type=MESH)
 
         pl.when((sectors * v + sec) // UNITS != sec)(lambda: arrival(0).wait_recv())
-        for j in range(1, peers):
+        for j in range(1, chips):
             arrival(j).wait_recv()
         total = rbuf[v, 0].astype(F32)
-        for j in range(1, peers):
+        for j in range(1, chips):
             total = total + rbuf[v, j].astype(F32)
         out_ref[v, 0] = total.astype(BF16)
 
@@ -258,7 +274,8 @@
 
         when(both if ch >= HALF else None, sent)
     for unit in range(UNITS):
-        for j in range(1, peers):
+        pair_copy(unit).wait_send()
+        for j in range(1, chips):
             reduce_copy(unit, j).wait_send()
         pl.when(unit_target[unit] != sec)(lambda: reduce_copy(unit, 0).wait_send())
 
@@ -272,11 +289,13 @@
     scratch = [pltpu.VMEM((8, size, width), BF16) for _ in range(chunks)] + [
         pltpu.VMEM((ops, size, size), BF16),
         pltpu.VMEM((ops, size, size), BF16),
-        pltpu.VMEM((2, size, size), F32),
-        pltpu.VMEM((UNITS, size, size), BF16),
-        pltpu.VMEM((vectors, 16, size // 16, size), BF16),
+        pltpu.VMEM((UNITS, 8, 2, size // 16, size), F32),
+        pltpu.VMEM((UNITS, 8, size // 16, size), BF16),
+        pltpu.VMEM((UNITS, 8, size // 16, size), BF16),
+        pltpu.VMEM((UNITS, 8, size // 16, size), BF16),
+        pltpu.VMEM((vectors, 8, size // 16, size), BF16),
         dma((chunks, 7)), dma((chunks, 7)), dma((chunks, 3)), dma((chunks, 3)), dma((chunks,)), dma((chunks,)),
-        dma((UNITS, 16)), dma((vectors, 16)), dma((2,)), dma((chunks,)), dma((1,)),
+        dma((UNITS,)), dma((UNITS,)), dma((UNITS, 8)), dma((vectors, 8)), dma((2,)), dma((chunks,)), dma((1,)),
     ]
     hbm = pl.BlockSpec(memory_space=pl.ANY)
     return pl.pallas_call(

time: 75.1 us -> 70.6 us (0.940); the launches traced: 73.8 us -> 70.4 us
  Pallas kernels: 70.9 us -> 67.5 us
    pallas_call x1, Pallas kernels: 70.9 us -> 67.5 us  [per_device(): pl.pallas_call(kernel, out_shape=jax.ShapeDtypeStruct((vectors, 1, size /...]
where the time goes in v3:
time: 70.6 us; the launch traced here: 70.4 us
  Pallas kernels  67.5 us (96%)
  local copies, waits for them, and re-layouts  2.89 us (4%)
    pallas_call x1, Pallas kernels, per_device(): pl.pallas_call(kernel, out_shape=jax.ShapeDtypeStruct((vectors, 1, size /...  67.5 us
    unnamed x2, local copies, waits for them, and re-layouts  2.89 us

profile of v3, /device:TPU:0, one launch (start us, length us, event | category | flops | bytes accessed | tf_op | source)
XLA Modules:
  0.0 70.4 jit_solution(13052727553770511476)
XLA Ops:
  0.0 1.4 %copy.5.targets = s32[16,8]{1,0:T(8,128)} copy(s32[16,8]{0,1:T(8,128)} %param.7) | data formatting | bytes 1024 | tf_op args[3]
  1.4 67.5 %sigma.1 = bf16[3,1,32,512]{3,2,1,0:T(8,128)(2,1)} custom-call(bf16[3,1,512,512]{3,2,1,0:T(8,128)(2,1)} %psi_hbm.1, bf16[16,512,512]{2,1,0:T(8,128)(2,1)} %left_hbm.1, bf16[16,512,512]{2,1,0:T(8,128)(2,1)} %right_hbm.1, s32[16,8]{1,0:T(8,128)} %copy.5.targets), custom_call_target="tpu_custom_call" | custom-call | tf_op jit(solution)/shard_map/sigma/pallas_call | solution.py:301
  68.9 1.5 %copy.7 = bf16[3,1,32,512]{3,2,1,0:T(8,128)(2,1)} copy(bf16[3,1,32,512]{3,2,1,0:T(8,128)(2,1)} %sigma.1) | data formatting | bytes 196608

commit v4 on v3

--- a/solution.py
+++ b/solution.py
@@ -11,6 +11,7 @@
 UNROLL = 4
 HALF = 2
 UNITS = 3
+SPLIT = 2
 
 
 def kernel(psi_hbm, left_hbm, right_hbm, targets, out_ref, *scratch):
@@ -64,8 +65,10 @@
     colour = lax.rem(y + 2 * zl, 4)
     base = core * rows_core
 
-    def shard_rows(q):
-        return pl.ds(pl.multiple_of(base + q * shard, 16), shard)
+    piece = shard // SPLIT
+
+    def shard_rows(q, g):
+        return pl.ds(pl.multiple_of(base + lax.rem(q, 4) * shard + g * piece, 16), piece)
 
     barrier = pltpu.get_barrier_semaphore()
     for dx, dz, _ in routes:
@@ -79,26 +82,33 @@
         cols = slice(h * width, (h + 1) * width)
         own_copies.append(pltpu.make_async_copy(
             psi_hbm.at[1 if is_b else vector_a(sec), 0, :, cols], bufs[ch].at[0], own_sem.at[ch]))
-        copies = []
-        for i, (dx, dz, slot) in enumerate(routes):
-            rows = shard_rows(lax.rem(colour + 2 * dz, 4))
-            peer = sec_peer(dx, dz)
-            copies.append((two_vectors(peer[1]) if is_b else None, pltpu.make_async_remote_copy(
-                src_ref=psi_hbm.at[1 if is_b else vector_a(peer[1]), 0, rows, cols],
-                dst_ref=bufs[ch].at[slot, rows, :],
-                send_sem=s1_send.at[ch, i], recv_sem=s1_recv.at[ch, i],
-                device_id=peer, device_id_type=MESH)))
-        first.append(copies)
-        rows = shard_rows(colour)
-        share.append([pltpu.make_async_remote_copy(
-            src_ref=bufs[ch].at[1:8, rows, :], dst_ref=bufs[ch].at[1:8, rows, :],
-            send_sem=sh_send.at[ch, i], recv_sem=sh_recv.at[ch, i],
-            device_id=(near[i], sec), device_id_type=MESH) for i in range(3)])
-        rows = pl.ds(pl.multiple_of(base, rows_core), rows_core)
-        cross.append(pltpu.make_async_remote_copy(
-            src_ref=bufs[ch].at[1:8, rows, :], dst_ref=bufs[ch].at[1:8, rows, :],
-            send_sem=mt_send.at[ch], recv_sem=mt_recv.at[ch],
-            device_id=(mate, sec), device_id_type=MESH))
+        first.append([])
+        share.append([])
+        cross.append([])
+        for g in range(SPLIT):
+            copies = []
+            for i, (dx, dz, slot) in enumerate(routes):
+                rows = shard_rows(colour + 2 * dz, g)
+                peer = sec_peer(dx, dz)
+                copies.append((two_vectors(peer[1]) if is_b else None, pltpu.make_async_remote_copy(
+                    src_ref=psi_hbm.at[1 if is_b else vector_a(peer[1]), 0, rows, cols],
+                    dst_ref=bufs[ch].at[slot, rows, :],
+                    send_sem=s1_send.at[ch, g, i], recv_sem=s1_recv.at[ch, g, i],
+                    device_id=peer, device_id_type=MESH)))
+            first[ch].append(copies)
+            rows = shard_rows(colour, g)
+            share[ch].append([pltpu.make_async_remote_copy(
+                src_ref=bufs[ch].at[1:8, rows, :], dst_ref=bufs[ch].at[1:8, rows, :],
+                send_sem=sh_send.at[ch, g, i], recv_sem=sh_recv.at[ch, g, i],
+                device_id=(near[i], sec), device_id_type=MESH) for i in range(3)])
+            copies = []
+            for n, q in enumerate((0, 3, 1, 2)):
+                rows = shard_rows(colour + q, g)
+                copies.append(pltpu.make_async_remote_copy(
+                    src_ref=bufs[ch].at[1:8, rows, :], dst_ref=bufs[ch].at[1:8, rows, :],
+                    send_sem=mt_send.at[ch, g, n], recv_sem=mt_recv.at[ch, g, n],
+                    device_id=(mate, sec), device_id_type=MESH))
+            cross[ch].append(copies)
     loads = [pltpu.make_async_copy(left_hbm, left, load_sem.at[0]),
              pltpu.make_async_copy(right_hbm, right, load_sem.at[1])]
 
@@ -109,22 +119,26 @@
             pl.when(condition)(action)
 
     def start_first(ch):
-        for condition, copy in first[ch]:
-            when(condition, copy.start)
-
-    def step_share(ch):
-        for _, copy in first[ch]:
+        for g in range(SPLIT):
+            for condition, copy in first[ch][g]:
+                when(condition, copy.start)
+
+    def step_share(ch, g):
+        for _, copy in first[ch][g]:
             copy.wait_recv()
-        for copy in share[ch]:
+        for copy in share[ch][g]:
             copy.start()
-
-    def step_cross(ch):
-        for copy in share[ch]:
-            copy.wait_recv()
-        cross[ch].start()
+        cross[ch][g][0].start()
+
+    def step_cross(ch, g):
+        for i in range(3):
+            share[ch][g][i].wait_recv()
+            cross[ch][g][i + 1].start()
 
     def step_ready(ch):
-        cross[ch].wait_recv()
+        for copies in cross[ch]:
+            for copy in copies:
+                copy.wait_recv()
         own_copies[ch].wait()
 
     own_copies[0].start()
@@ -132,13 +146,8 @@
     for copy in loads:
         copy.start()
     pl.semaphore_wait(barrier, len(routes) + peers - 1)
-    for ch in range(chunks):
-        start_first(ch)
-
-    @pl.when(both)
-    def _():
-        own_copies[2].start()
-        own_copies[3].start()
+    start_first(0)
+    start_first(1)
 
     def slot_of(k, target):
         source = jnp.int32(0)
@@ -204,25 +213,43 @@
         pl.when(jnp.logical_not(mine))(lambda: reduce_copy(unit, 0).start())
         pl.when(mine)(lambda: keep_copy(unit).start())
 
-    step_share(0)
-    step_share(1)
-    step_cross(0)
+    step_share(0, 0)
+    step_share(0, 1)
+    step_share(1, 0)
+    step_cross(0, 0)
+    step_share(1, 1)
+    step_cross(0, 1)
+    start_first(2)
+    start_first(3)
+
+    @pl.when(both)
+    def _():
+        own_copies[2].start()
+        own_copies[3].start()
+
     for copy in loads:
         copy.wait()
     step_ready(0)
     compute(0, 0)
-    step_cross(1)
+    for g in range(SPLIT):
+        step_cross(1, g)
 
     @pl.when(both)
     def _():
-        step_share(2)
-        step_share(3)
+        for ch in (2, 3):
+            for g in range(SPLIT):
+                step_share(ch, g)
 
     compute(1, 0)
     step_ready(1)
     compute(0, 1)
     send_pair(0)
-    pl.when(both)(lambda: step_cross(2))
+
+    @pl.when(both)
+    def _():
+        for g in range(SPLIT):
+            step_cross(2, g)
+
     compute(1, 1, 0, ops // 2)
     send(0)
     compute(1, 1, ops // 2)
@@ -230,7 +257,8 @@
 
     @pl.when(both)
     def _():
-        step_cross(3)
+        for g in range(SPLIT):
+            step_cross(3, g)
         step_ready(2)
         compute(2, 2)
         send(1)
@@ -265,12 +293,14 @@
         out_ref[v, 0] = total.astype(BF16)
 
     for ch in range(chunks):
-        for condition, copy in first[ch]:
-            when(condition, copy.wait_send)
+        for g in range(SPLIT):
+            for condition, copy in first[ch][g]:
+                when(condition, copy.wait_send)
 
         def sent():
-            for copy in share[ch] + [cross[ch]]:
-                copy.wait_send()
+            for g in range(SPLIT):
+                for copy in share[ch][g] + cross[ch][g]:
+                    copy.wait_send()
 
         when(both if ch >= HALF else None, sent)
     for unit in range(UNITS):
@@ -294,7 +324,8 @@
         pltpu.VMEM((UNITS, 8, size // 16, size), BF16),
         pltpu.VMEM((UNITS, 8, size // 16, size), BF16),
         pltpu.VMEM((vectors, 8, size // 16, size), BF16),
-        dma((chunks, 7)), dma((chunks, 7)), dma((chunks, 3)), dma((chunks, 3)), dma((chunks,)), dma((chunks,)),
+        dma((chunks, SPLIT, 7)), dma((chunks, SPLIT, 7)), dma((chunks, SPLIT, 3)), dma((chunks, SPLIT, 3)),
+        dma((chunks, SPLIT, 4)), dma((chunks, SPLIT, 4)),
         dma((UNITS,)), dma((UNITS,)), dma((UNITS, 8)), dma((vectors, 8)), dma((2,)), dma((chunks,)), dma((1,)),
     ]
     hbm = pl.BlockSpec(memory_space=pl.ANY)

time: 70.6 us -> 71.3 us (level)
  no operation moved by 1% of the time
where the time goes in v4:
time: 71.3 us; the launch traced here: 70.5 us
  Pallas kernels  67.6 us (95%)
  local copies, waits for them, and re-layouts  2.89 us (4%)
    pallas_call x1, Pallas kernels, per_device(): pl.pallas_call(kernel, out_shape=jax.ShapeDtypeStruct((vectors, 1, size /...  67.6 us
    unnamed x2, local copies, waits for them, and re-layouts  2.89 us

profile of v4, /device:TPU:0, one launch (start us, length us, event | category | flops | bytes accessed | tf_op | source)
XLA Modules:
  0.0 70.5 jit_solution(12489993731089061411)
XLA Ops:
  0.0 1.4 %copy.5.targets = s32[16,8]{1,0:T(8,128)} copy(s32[16,8]{0,1:T(8,128)} %param.7) | data formatting | bytes 1024 | tf_op args[3]
  1.4 67.6 %sigma.1 = bf16[3,1,32,512]{3,2,1,0:T(8,128)(2,1)} custom-call(bf16[3,1,512,512]{3,2,1,0:T(8,128)(2,1)} %psi_hbm.1, bf16[16,512,512]{2,1,0:T(8,128)(2,1)} %left_hbm.1, bf16[16,512,512]{2,1,0:T(8,128)(2,1)} %right_hbm.1, s32[16,8]{1,0:T(8,128)} %copy.5.targets), custom_call_target="tpu_custom_call" | custom-call | tf_op jit(solution)/shard_map/sigma/pallas_call | solution.py:332
  69.0 1.5 %copy.7 = bf16[3,1,32,512]{3,2,1,0:T(8,128)(2,1)} copy(bf16[3,1,32,512]{3,2,1,0:T(8,128)(2,1)} %sigma.1) | data formatting | bytes 196608

commit v5 on v4

--- a/solution.py
+++ b/solution.py
@@ -8,7 +8,7 @@
 F32 = jnp.float32
 BF16 = jnp.bfloat16
 MESH = pl.DeviceIdType.MESH
-UNROLL = 4
+UNROLL = 8
 HALF = 2
 UNITS = 3
 SPLIT = 2
@@ -143,10 +143,10 @@
 
     own_copies[0].start()
     own_copies[1].start()
+    pl.semaphore_wait(barrier, len(routes) + peers - 1)
+    start_first(0)
     for copy in loads:
         copy.start()
-    pl.semaphore_wait(barrier, len(routes) + peers - 1)
-    start_first(0)
     start_first(1)
 
     def slot_of(k, target):

time: 71.3 us -> 70.2 us (0.985)
  Pallas kernels: 67.6 us -> 66.1 us
    pallas_call x1, Pallas kernels: 67.6 us -> 66.1 us  [per_device(): pl.pallas_call(kernel, out_shape=jax.ShapeDtypeStruct((vectors, 1, size /...]
where the time goes in v5:
time: 70.2 us; the launch traced here: 69.1 us
  Pallas kernels  66.1 us (94%)
  local copies, waits for them, and re-layouts  2.89 us (4%)
    pallas_call x1, Pallas kernels, per_device(): pl.pallas_call(kernel, out_shape=jax.ShapeDtypeStruct((vectors, 1, size /...  66.1 us
    unnamed x2, local copies, waits for them, and re-layouts  2.89 us

profile of v5, /device:TPU:0, one launch (start us, length us, event | category | flops | bytes accessed | tf_op | source)
XLA Modules:
  0.0 69.1 jit_solution(10402712991717750435)
XLA Ops:
  0.0 1.4 %copy.5.targets = s32[16,8]{1,0:T(8,128)} copy(s32[16,8]{0,1:T(8,128)} %param.7) | data formatting | bytes 1024 | tf_op args[3]
  1.4 66.1 %sigma.1 = bf16[3,1,32,512]{3,2,1,0:T(8,128)(2,1)} custom-call(bf16[3,1,512,512]{3,2,1,0:T(8,128)(2,1)} %psi_hbm.1, bf16[16,512,512]{2,1,0:T(8,128)(2,1)} %left_hbm.1, bf16[16,512,512]{2,1,0:T(8,128)(2,1)} %right_hbm.1, s32[16,8]{1,0:T(8,128)} %copy.5.targets), custom_call_target="tpu_custom_call" | custom-call | tf_op jit(solution)/shard_map/sigma/pallas_call | solution.py:332
  67.5 1.5 %copy.7 = bf16[3,1,32,512]{3,2,1,0:T(8,128)(2,1)} copy(bf16[3,1,32,512]{3,2,1,0:T(8,128)(2,1)} %sigma.1) | data formatting | bytes 196608
